TPU v7x, 32 devices: a whole 2x2x4 slice. The times are simulated.
32 devices in a mesh: point: 8 (over y, x, core), batch: 4 (over z).
Axes of the slice: x: 2, y: 2, z: 4, core: 2. Of those that a mesh axis runs over, the one named last changes fastest.
Arguments:
- activations: bfloat16 [128, 14, 14, 1024], P('batch'), may hold values from -8 to 8
- labels: int32 [128], P('batch'), may hold values from 0 to 999
- t_values: float32 [64], replicated, may hold values from 0 to 1
- point_index: int32 [8], replicated, may hold values from 0 to 63
- w_reduce: bfloat16 [3, 1024, 256], P(None, 'point'), may hold values from -1 to 1
- w_spatial: bfloat16 [3, 2304, 256], P(None, 'point'), may hold values from -0.125 to 0.125
- w_expand: bfloat16 [3, 256, 1024], P(None, 'point'), may hold values from -0.375 to 0.375
- w_classes: bfloat16 [3, 1000, 1024], P(None, None, 'point'), may hold values from -0.1875 to 0.1875
- norm_gain: float32 [3, 1536], replicated, may hold values from 0.5 to 1.5
- norm_bias: float32 [3, 1536], replicated, may hold values from -3 to 3
- class_bias: float32 [3, 1000], replicated, may hold values from -3 to 3
Outputs:
- mean_reduce: float32 [8, 256], P('point')
- var_reduce: float32 [8, 256], P('point')
- mean_spatial: float32 [8, 256], P('point')
- var_spatial: float32 [8, 256], P('point')
- mean_expand: float32 [8, 1024], P('point')
- var_expand: float32 [8, 1024], P('point')
- margin: float32 [8], replicated
All inputs are finite; a program needn't handle non-finite values.
Results may differ from a plain program's by a relative error of at most 0.003.
Values may be sent and summed in bfloat16 or wider, within the bound.
A program may use at most 128 MiB of HBM per device.

v0:
```python
import jax
import jax.numpy as jnp
from jax import lax
from jax.sharding import PartitionSpec as P

EPSILON = 1e-05


def curve_coefficients(t_values, point_index):
    table_size = t_values.shape[0]
    matches = point_index[:, None] == jnp.arange(table_size, dtype=jnp.int32)[None, :]
    picked = jnp.sum(jnp.where(matches, t_values[None, :], 0.0), axis=1)
    doubled = 2.0 * picked
    return jnp.stack(
        [
            jnp.maximum(1.0 - doubled, 0.0),
            1.0 - jnp.abs(1.0 - doubled),
            jnp.maximum(doubled - 1.0, 0.0),
        ],
        axis=1,
    )


def blend_all(coefficients, endpoints):
    target_shape = (coefficients.shape[0],) + (1,) * (endpoints.ndim - 1)
    start_part = coefficients[:, 0].reshape(target_shape) * endpoints[0].astype(jnp.float32)[None]
    bend_part = coefficients[:, 1].reshape(target_shape) * endpoints[1].astype(jnp.float32)[None]
    final_part = coefficients[:, 2].reshape(target_shape) * endpoints[2].astype(jnp.float32)[None]
    return start_part + bend_part + final_part


def point_weight(endpoints, own_row, by_columns):
    if by_columns:
        gathered = lax.all_gather(endpoints, "point", axis=2, tiled=True)
    else:
        gathered = lax.all_gather(endpoints, "point", axis=1, tiled=True)
    return blend_all(own_row, gathered)[0].astype(jnp.bfloat16)


def map_product(maps, kernel):
    return lax.dot_general(
        maps, kernel, (((3,), (0,)), ((), ())), preferred_element_type=jnp.float32
    )


def batch_norm(pre_norm, gain_part, bias_part, row_count):
    channel_total, channel_squares = lax.psum(
        (jnp.sum(pre_norm, axis=(0, 1, 2)), jnp.sum(pre_norm * pre_norm, axis=(0, 1, 2))), "batch"
    )
    channel_mean = channel_total / row_count
    channel_var = channel_squares / row_count - channel_mean * channel_mean
    scaled = (pre_norm - channel_mean) * lax.rsqrt(channel_var + EPSILON) * gain_part + bias_part
    return (channel_mean, channel_var, scaled)


def spatial_conv(source, kernel):
    side_len = source.shape[1]
    middle = source.shape[3]
    padded = jnp.pad(source, ((0, 0), (1, 1), (1, 1), (0, 0)))
    widened = jnp.concatenate(
        [
            padded[:, :, 0:side_len, :],
            padded[:, :, 1 : side_len + 1, :],
            padded[:, :, 2 : side_len + 2, :],
        ],
        axis=3,
    )
    summed = map_product(widened[:, 0:side_len], kernel[0 : 3 * middle])
    summed = summed + map_product(widened[:, 1 : side_len + 1], kernel[3 * middle : 6 * middle])
    summed = summed + map_product(widened[:, 2 : side_len + 2], kernel[6 * middle : 9 * middle])
    return summed


def shards(
    activations,
    labels,
    t_values,
    point_index,
    w_reduce,
    w_spatial,
    w_expand,
    w_classes,
    norm_gain,
    norm_bias,
    class_bias,
):
    coefficients = curve_coefficients(t_values, point_index)
    own_row = lax.dynamic_slice_in_dim(coefficients, lax.axis_index("point"), 1, 0)
    reduce_w = point_weight(w_reduce, own_row, False)
    spatial_w = point_weight(w_spatial, own_row, False)
    expand_w = point_weight(w_expand, own_row, False)
    class_w = point_weight(w_classes, own_row, True)
    gain_now = blend_all(own_row, norm_gain)[0]
    bias_now = blend_all(own_row, norm_bias)[0]
    shift_now = blend_all(own_row, class_bias)[0]
    images, side_len, _, channels = activations.shape
    middle = w_reduce.shape[2]
    row_count = float(images * side_len * side_len * lax.axis_size("batch"))
    reduced = map_product(activations, reduce_w)
    mean_one, var_one, normed_one = batch_norm(
        reduced, gain_now[:middle], bias_now[:middle], row_count
    )
    first = jax.nn.relu(normed_one).astype(jnp.bfloat16)
    spatial = spatial_conv(first, spatial_w)
    mean_two, var_two, normed_two = batch_norm(
        spatial, gain_now[middle : 2 * middle], bias_now[middle : 2 * middle], row_count
    )
    second = jax.nn.relu(normed_two).astype(jnp.bfloat16)
    expanded = map_product(second, expand_w)
    mean_three, var_three, normed_three = batch_norm(
        expanded, gain_now[2 * middle :], bias_now[2 * middle :], row_count
    )
    block_out = jax.nn.relu(normed_three + activations.astype(jnp.float32))
    pooled = jnp.mean(block_out, axis=(1, 2)).astype(jnp.bfloat16)
    logits = (
        lax.dot_general(
            pooled, class_w, (((1,), (1,)), ((), ())), preferred_element_type=jnp.float32
        )
        + shift_now
    )
    classes = logits.shape[1]
    onehot = labels[:, None] == jnp.arange(classes, dtype=jnp.int32)[None, :]
    correct = jnp.sum(jnp.where(onehot, logits, 0.0), axis=1)
    rivals = jnp.max(jnp.where(onehot, -1e30, logits), axis=1)
    partial_value = jnp.sum(correct - rivals) / (images * lax.axis_size("batch"))
    point_count = point_index.shape[0]
    placed = jnp.where(
        jnp.arange(point_count, dtype=jnp.int32) == lax.axis_index("point"), partial_value, 0.0
    )
    margin_all = lax.psum(placed, ("point", "batch"))
    return (
        mean_one[None],
        var_one[None],
        mean_two[None],
        var_two[None],
        mean_three[None],
        var_three[None],
        margin_all,
    )


def solution(mesh):
    placed = (
        P("batch", None, None, None),
        P("batch"),
        P(),
        P(),
        P(None, "point", None),
        P(None, "point", None),
        P(None, "point", None),
        P(None, None, "point"),
        P(),
        P(),
        P(),
    )
    return jax.shard_map(
        shards,
        mesh=mesh,
        in_specs=placed,
        out_specs=(
            P("point", None),
            P("point", None),
            P("point", None),
            P("point", None),
            P("point", None),
            P("point", None),
            P(),
        ),
        check_vma=False,
    )
```

profile of v0, /device:TPU:0, one launch (start us, length us, event | category | flops | bytes accessed | tf_op | source)
XLA Modules:
  0.0 208.5 jit_solution(10090536275269189656)
XLA Ops:
  7.2 0.7 all-gather.5.cloned.1.call-update
  7.9 0.7 all-gather.7.cloned.1.call-update
  8.7 0.7 all-gather.9.cloned.1.call-update
  10.0 0.9 select_reduce_fusion.2
  11.5 2.8 %multiply_add_fusion = (f32[1,1536]{1,0:T(1,128)S(1)}, f32[1,1536]{1,0:T(1,128)S(1)}) fusion(f32[3,1536]{1,0:T(4,128)} %param.20, f32[]{:T(128)} %bitcast.5, f32[]{:T(128)} %bitcast.4, f32[]{:T(128)} %bitcast.3, f32[3,1536]{1,0:T(4,128)} %param.19), kind=kLoop, calls=%fused_computation.50 | loop fusion | flops 15360 | bytes 49164 | tf_op jit(solution)/shard_map/add | solution.py:29
  14.3 2.7 %multiply_add_fusion.2 = f32[1,1000]{1,0:T(1,128)S(1)} fusion(f32[3,1000]{1,0:T(4,128)} %param.21, f32[]{:T(128)} %bitcast.5, f32[]{:T(128)} %bitcast.4, f32[]{:T(128)} %bitcast.3), kind=kLoop, calls=%fused_computation.52 | loop fusion | flops 5000 | bytes 16012 | tf_op jit(solution)/shard_map/add | solution.py:29
  17.0 21.2 %all-gather.5.cloned.1.call-done = bf16[3,1024,256]{2,1,0:T(8,128)(2,1)} async-done(((bf16[3,128,256]{2,1,0:T(8,128)(2,1)}), bf16[3,1024,256]{2,1,0:T(8,128)(2,1)}) %all-gather.5.cloned.1.call-update) | async-done | bytes 1572880 | tf_op jit(solution)/shard_map/all_gather | solution.py:36
  38.2 13.3 %multiply_reduce_fusion.2 = (f32[256]{0:T(256)S(1)}, f32[256]{0:T(256)S(1)}, f32[256,32,14,14]{0,1,3,2:T(8,128)}) fusion(bf16[32,14,14,1024]{3,0,2,1:T(8,128)(2,1)} %param.11, bf16[3,1024,256]{2,1,0:T(8,128)(2,1)} %all-gather.5.cloned.1.call-done, f32[]{:T(128)} %bitcast.5, f32[]{:T(128)} %bitcast.4, f32[]{:T(128)} %bitcast.3), kind=kOutput, calls=%fused_computation.7 | convolution fusion | flops 3295510016 | bytes 20842508 | tf_op jit(solution)/shard_map/dot_general | solution.py:41
  51.5 11.7 %all-reduce.3 = (f32[256]{0:T(256)S(1)}, f32[256]{0:T(256)S(1)}) all-reduce(f32[256]{0:T(256)S(1)} %get-tuple-element.12, f32[256]{0:T(256)S(1)} %get-tuple-element.11), channel_id=1, replica_groups=mesh['point'=8,'batch'=4] {'batch'}, use_global_device_ids=true, to_apply=%region_2.3 | all-reduce | flops 512 | bytes 4096 | tf_op jit(solution)/shard_map/psum | solution.py:47
  63.8 4.1 %fusion.1 = bf16[32,14,14,256]{3,0,2,1:T(8,128)(2,1)S(1)} fusion(f32[256,32,14,14]{0,1,3,2:T(8,128)} %get-tuple-element.43, f32[256]{0:T(256)S(1)} %bitcast.77, f32[256]{0:T(256)S(1)} %bitcast.78, f32[256]{0:T(256)S(1)} %get-tuple-element.25, f32[256]{0:T(256)S(1)} %get-tuple-element.39), kind=kLoop, calls=%fused_computation.13 | loop fusion | flops 9633792 | bytes 9637888 | tf_op jit(solution)/shard_map/convert_element_type | solution.py:103
  67.9 4.9 %pad_slice_fusion.2 = (bf16[32,16,14,256]{3,0,2,1:T(8,128)(2,1)}, bf16[32,16,14,256]{3,0,2,1:T(8,128)(2,1)}, bf16[32,16,14,256]{3,0,2,1:T(8,128)(2,1)}) fusion(bf16[32,14,14,256]{3,0,2,1:T(8,128)(2,1)S(1)} %fusion.1), kind=kLoop, calls=%fused_computation.10 | loop fusion | bytes 14221312 | tf_op jit(solution)/shard_map/slice | solution.py:62
  72.8 1.2 all-gather.7.cloned.1.call-done
  74.0 4.5 %add_convert_fusion.1 = bf16[1,2304,256]{2,1,0:T(8,128)(2,1)S(1)} fusion(bf16[3,2304,256]{2,1,0:T(8,128)(2,1)} %all-gather.7.cloned.1.call-done, f32[]{:T(128)} %bitcast.5, f32[]{:T(128)} %bitcast.4, f32[]{:T(128)} %bitcast.3), kind=kLoop, calls=%fused_computation.19 | loop fusion | flops 5308416 | bytes 4718604 | tf_op jit(solution)/shard_map/convert_element_type | solution.py:37
  78.5 7.3 %fusion.31 = f32[32,14,14,256]{3,0,2,1:T(8,128)} fusion(bf16[1,2304,256]{2,1,0:T(8,128)(2,1)S(1)} %add_convert_fusion.1, bf16[32,16,14,256]{3,0,2,1:T(8,128)(2,1)} %get-tuple-element.29, bf16[32,16,14,256]{3,0,2,1:T(8,128)(2,1)} %get-tuple-element.28, bf16[32,16,14,256]{3,0,2,1:T(8,128)(2,1)} %get-tuple-element.27), kind=kOutput, calls=%fused_computation.44 | convolution fusion | flops 2499280896 | bytes 17825792 | tf_op jit(solution)/shard_map/dot_general | solution.py:41
  85.8 1.2 copy-done.1
  87.0 1.0 copy-done.2
  88.0 5.4 %fusion.30 = f32[32,14,14,256]{3,0,2,1:T(8,128)} fusion(bf16[1,2304,256]{2,1,0:T(8,128)(2,1)S(1)} %add_convert_fusion.1, bf16[32,16,14,256]{3,0,2,1:T(8,128)(2,1)S(1)} %copy-done.2, bf16[32,16,14,256]{3,0,2,1:T(8,128)(2,1)S(1)} %copy-done.1, bf16[32,16,14,256]{3,0,2,1:T(8,128)(2,1)S(1)} %copy-done), kind=kOutput, calls=%fused_computation.42 | convolution fusion | flops 2499280896 | bytes 17825792 | tf_op jit(solution)/shard_map/dot_general | solution.py:41
  93.4 9.0 %multiply_reduce_fusion.1 = (f32[256]{0:T(256)S(1)}, f32[256]{0:T(256)S(1)}, f32[32,14,14,256]{3,0,2,1:T(8,128)}) fusion(bf16[1,2304,256]{2,1,0:T(8,128)(2,1)S(1)} %add_convert_fusion.1, bf16[32,16,14,256]{3,0,2,1:T(8,128)(2,1)S(1)} %copy-done.2, bf16[32,16,14,256]{3,0,2,1:T(8,128)(2,1)S(1)} %copy-done.1, bf16[32,16,14,256]{3,0,2,1:T(8,128)(2,1)S(1)} %copy-done, ...), kind=kOutput, calls=%fused_computation.5 | convolution fusion | flops 2507308544 | bytes 30672896 | tf_op jit(solution)/shard_map/dot_general | solution.py:41
  102.4 11.9 %all-reduce.2 = (f32[256]{0:T(256)S(1)}, f32[256]{0:T(256)S(1)}) all-reduce(f32[256]{0:T(256)S(1)} %get-tuple-element.10, f32[256]{0:T(256)S(1)} %get-tuple-element.9), channel_id=1, replica_groups=mesh['point'=8,'batch'=4] {'batch'}, use_global_device_ids=true, to_apply=%region_6.7 | all-reduce | flops 512 | bytes 4096 | tf_op jit(solution)/shard_map/psum | solution.py:47
  114.9 16.0 %multiply_reduce_fusion = (f32[1024]{0:T(1024)S(1)}, f32[1024]{0:T(1024)S(1)}, f32[32,14,14,1024]{3,0,2,1:T(8,128)}) fusion(bf16[3,256,1024]{2,1,0:T(8,128)(2,1)} %all-gather.9.cloned.1.call-done, f32[]{:T(128)} %bitcast.5, f32[]{:T(128)} %bitcast.4, f32[]{:T(128)} %bitcast.3, f32[32,14,14,256]{3,0,2,1:T(8,128)} %get-tuple-element.44, f32[256]{0:T(256)S(1)} %bitcast.84, ...), kind=kOutput, calls=%fused_computation.1 | convolution fusion | flops 3319592960 | bytes 33697804 | tf_op jit(solution)/shard_map/dot_general | solution.py:41
  130.9 8.5 %all-reduce.1 = (f32[1024]{0:T(1024)S(1)}, f32[1024]{0:T(1024)S(1)}) all-reduce(f32[1024]{0:T(1024)S(1)} %get-tuple-element.8, f32[1024]{0:T(1024)S(1)} %get-tuple-element.7), channel_id=1, replica_groups=mesh['point'=8,'batch'=4] {'batch'}, use_global_device_ids=true, to_apply=%region_10.11 | all-reduce | flops 2048 | bytes 16384 | tf_op jit(solution)/shard_map/psum | solution.py:47
  140.1 14.9 %maximum_reduce_fusion = f32[32,1024]{1,0:T(8,128)S(1)} fusion(bf16[32,14,14,1024]{3,0,2,1:T(8,128)(2,1)} %param.11, f32[32,14,14,1024]{3,0,2,1:T(8,128)} %get-tuple-element.45, f32[1024]{0:T(1024)S(1)} %bitcast.74, f32[1024]{0:T(1024)S(1)} %bitcast.75, f32[1024]{0:T(1024)S(1)} %get-tuple-element.21, f32[1024]{0:T(1024)S(1)} %get-tuple-element.34), kind=kLoop, calls=%fused_computation | loop fusion | flops 51347456 | bytes 38682624 | tf_op jit(solution)/shard_map/reduce_sum | solution.py:114
  155.0 6.1 %select_reduce_fusion = (f32[32]{0:T(128)S(1)}, f32[32]{0:T(128)S(1)}) fusion(s32[32]{0:T(128)S(1)} %copy-done.6, f32[1000]{0:T(1024)S(1)} %bitcast.80, bf16[3,1000,1024]{2,1,0:T(8,128)(2,1)} %all-gather.11.cloned.1.call-done, f32[]{:T(128)} %bitcast.5, f32[]{:T(128)} %bitcast.4, f32[]{:T(128)} %bitcast.3, f32[32,1024]{1,0:T(8,128)S(1)} %maximum_reduce_fusion), kind=kOutput, calls=%fused_computation.45 | convolution fusion | flops 75009472 | bytes 6279468 | tf_op jit(solution)/shard_map/dot_general | solution.py:116
  162.4 39.6 %psum.55 = f32[8]{0:T(128)} all-reduce(f32[8]{0:T(128)S(1)} %compare_select_fusion), channel_id=1, replica_groups=mesh['point'=8,'batch'=4] {'point','batch'}, use_global_device_ids=true, to_apply=%region_17.18 | all-reduce | flops 8 | bytes 64 | tf_op jit(solution)/shard_map/psum | solution.py:130
  (32 shorter events, 3.7 us)
Async XLA Ops:
  7.2 31.0 %all-gather.5.cloned.1.call-start = ((), (), s32[]{:S(2)}) async-start(), calls=%async_computation | async-start | bytes 1769472 | tf_op jit(solution)/shard_map/all_gather | solution.py:36
  7.9 66.1 %all-gather.7.cloned.1.call-start = ((), (), s32[]{:S(2)}) async-start(), calls=%async_computation.1 | async-start | bytes 3981312 | tf_op jit(solution)/shard_map/all_gather | solution.py:36
  8.7 106.3 %all-gather.9.cloned.1.call-start = ((), (), s32[]{:S(2)}) async-start(), calls=%async_computation.2 | async-start | bytes 1769472 | tf_op jit(solution)/shard_map/all_gather | solution.py:36
  9.4 145.6 %all-gather.11.cloned.1.call-start = ((), (), s32[]{:S(2)}) async-start(), calls=%async_computation.3 | async-start | bytes 6912000 | tf_op jit(solution)/shard_map/all_gather | solution.py:34
  63.8 9.0 %copy-start.4 = (f32[256]{0:T(256)}, f32[256]{0:T(256)S(1)}, u32[]{:S(2)}) copy-start(f32[256]{0:T(256)S(1)} %get-tuple-element.39) | copy-start | bytes 3076
  78.5 7.3 %copy-start = (bf16[32,16,14,256]{3,0,2,1:T(8,128)(2,1)S(1)}, bf16[32,16,14,256]{3,0,2,1:T(8,128)(2,1)}, u32[]{:S(2)}) copy-start(bf16[32,16,14,256]{3,0,2,1:T(8,128)(2,1)} %get-tuple-element.27) | copy-start | bytes 11010052
  78.5 8.5 %copy-start.1 = (bf16[32,16,14,256]{3,0,2,1:T(8,128)(2,1)S(1)}, bf16[32,16,14,256]{3,0,2,1:T(8,128)(2,1)}, u32[]{:S(2)}) copy-start(bf16[32,16,14,256]{3,0,2,1:T(8,128)(2,1)} %get-tuple-element.28) | copy-start | bytes 11010052
  78.5 9.5 %copy-start.2 = (bf16[32,16,14,256]{3,0,2,1:T(8,128)(2,1)S(1)}, bf16[32,16,14,256]{3,0,2,1:T(8,128)(2,1)}, u32[]{:S(2)}) copy-start(bf16[32,16,14,256]{3,0,2,1:T(8,128)(2,1)} %get-tuple-element.29) | copy-start | bytes 11010052
  114.9 16.0 %copy-start.5 = (f32[256]{0:T(256)}, f32[256]{0:T(256)S(1)}, u32[]{:S(2)}) copy-start(f32[256]{0:T(256)S(1)} %get-tuple-element.38) | copy-start | bytes 3076
  140.1 14.9 %copy-start.3 = (f32[1024]{0:T(1024)}, f32[1024]{0:T(1024)S(1)}, u32[]{:S(2)}) copy-start(f32[1024]{0:T(1024)S(1)} %get-tuple-element.34) | copy-start | bytes 12292
  140.1 14.9 %copy-start.6 = (s32[32]{0:T(128)S(1)}, s32[32]{0:T(128)}, u32[]{:S(2)}) copy-start(s32[32]{0:T(128)} %param.12) | copy-start | bytes 388
Sparse Core Ops, SparseCore 0:
  9.9 28.2 all-gather.4
  40.1 33.8 all-gather.6
  75.9 25.5 all-gather.8
  103.2 45.9 all-gather.10
where the time goes:
time: 209 us; the launch traced here: 208 us
  blocking collectives  71.7 us (34%)
  matrix products  57.1 us (27%)
  other arithmetic  32.2 us (15%)
  waiting for transfers between devices  24.9 us (12%)
  between operations  14.6 us (7%)
  local copies, waits for them, and re-layouts  7.82 us (4%)
    dot_general x5, matrix products, map_product(): lax.dot_general(maps, kernel, (((3,), (0,)), ((), ())), preferred_element...  51 us
    psum x1, blocking collectives, shards(): margin_all = lax.psum(placed, ('point', 'batch'))  39.6 us
    psum x3, blocking collectives, batch_norm(): lax.psum((jnp.sum(pre_norm, axis=(0, 1, 2)), jnp.sum(pre_norm * pre_norm,...  32.1 us
    all_gather x3, waiting for transfers between devices, point_weight(): gathered = lax.all_gather(endpoints, 'point', axis=1, tiled=True)  22.3 us
    reduce_sum x1, other arithmetic, shards(): pooled = jnp.mean(block_out, axis=(1, 2)).astype(jnp.bfloat16)  14.9 us
    dot_general x1, matrix products, shards(): lax.dot_general(pooled, class_w, (((1,), (1,)), ((), ())), preferred_elem...  6.09 us
    add x2, other arithmetic, blend_all(): return start_part + bend_part + final_part  5.52 us
    slice x1, local copies, waits for them, and re-layouts, spatial_conv(): padded[:, :, 0:side_len, :]  4.94 us
  transfers between devices with their start and end apart: 4, of which 2 were waited for; matrix products, arithmetic and copies ran while one was open for 42% of the time, Pallas kernels for 0%

commit v1 on v0

v1 whole, which is shorter than its diff:
```python
import functools
import math

import jax
import jax.numpy as jnp
from jax import lax
from jax.experimental import pallas as pl
from jax.experimental.pallas import tpu as pltpu
from jax.sharding import PartitionSpec as P

EPSILON = 1e-05
MESH = pl.DeviceIdType.MESH
BF16 = jnp.bfloat16
F32 = jnp.float32


def round_up(value, step):
    return (value + step - 1) // step * step


def block_of(side):
    return 2 if side % 2 == 0 else 1


def dot(a, b, dims=((1,), (0,))):
    return lax.dot_general(a, b, (dims, ((), ())), preferred_element_type=F32)


def kernel(
    cfg,
    t_ref,
    index_ref,
    labels_ref,
    gain_ref,
    bias_ref,
    shift_ref,
    act_hbm,
    wr_hbm,
    ws_hbm,
    we_hbm,
    wc_hbm,
    mean1_out,
    var1_out,
    mean2_out,
    var2_out,
    mean3_out,
    var3_out,
    margin_out,
    act,
    anchor_r,
    anchor_s,
    anchor_e,
    anchor_c,
    send_r,
    send_s,
    send_e,
    send_c,
    recv_r,
    recv_s,
    recv_e,
    recv_c,
    rows_f32,
    wide,
    second,
    pooled_f32,
    pooled_all,
    stat1,
    stat2,
    stat3,
    label_all,
    score,
    margins,
    local_sem,
    act_sem,
    wsend,
    wrecv,
    zsend,
    zrecv,
    msend,
    mrecv,
):
    n, nb, images, side, cin, mid, classes, chunk, step = cfg
    blocks = side // step
    rows = step * side * images
    me = lax.axis_index("point")
    zz = lax.axis_index("batch")
    count = float(images * side * side * nb)
    start = jnp.minimum(zz * chunk, classes - chunk)
    start = pl.multiple_of(start, 8)

    barrier = pltpu.get_barrier_semaphore()
    for k in range(1, n):
        pl.semaphore_signal(
            barrier, inc=1, device_id=(lax.rem(me + k, n), zz), device_id_type=MESH
        )
    for k in range(1, nb):
        pl.semaphore_signal(
            barrier, inc=1, device_id=(me, lax.rem(zz + k, nb)), device_id_type=MESH
        )

    anchor_copies = []
    for i, (src, dst) in enumerate(
        (
            (wr_hbm, anchor_r),
            (ws_hbm, anchor_s),
            (we_hbm, anchor_e),
            (wc_hbm.at[:, pl.ds(start, chunk), :], anchor_c),
        )
    ):
        copy = pltpu.make_async_copy(src, dst, local_sem.at[i])
        copy.start()
        anchor_copies.append(copy)
    act_copies = []
    for b in range(blocks):
        copy = pltpu.make_async_copy(
            act_hbm.at[pl.ds(b * step, step)],
            act.at[pl.ds(b * step, step)],
            act_sem.at[b],
        )
        copy.start()
        act_copies.append(copy)

    def coefficients(point):
        doubled = 2.0 * t_ref[index_ref[point]]
        return (
            jnp.maximum(1.0 - doubled, 0.0),
            1.0 - jnp.abs(1.0 - doubled),
            jnp.maximum(doubled - 1.0, 0.0),
        )

    targets = [lax.rem(me + k, n) for k in range(n)]
    coefs = [coefficients(q) for q in targets]
    own = coefs[0]

    def blend(ends, c):
        return c[0] * ends[0] + c[1] * ends[1] + c[2] * ends[2]

    sends = []
    weights = (
        (anchor_r, send_r, recv_r),
        (anchor_s, send_s, recv_s),
        (anchor_e, send_e, recv_e),
        (anchor_c, send_c, recv_c),
    )
    for w, (anchor, send, recv) in enumerate(weights):
        anchor_copies[w].wait()
        total = anchor.shape[1]
        piece = 32 if total % 32 == 0 else 8

        def one(j, carry, anchor=anchor, send=send, recv=recv, piece=piece):
            at = pl.ds(pl.multiple_of(j * piece, piece), piece)
            ends = [anchor[a, at, :].astype(F32) for a in range(3)]
            for k in range(1, n):
                send[k - 1, at, :] = blend(ends, coefs[k]).astype(BF16)
            recv[me, at, :] = blend(ends, own).astype(BF16)
            return carry

        lax.fori_loop(0, total // piece, one, 0)
        if w == 0:
            pl.semaphore_wait(barrier, n - 1 + nb - 1)
        copies = []
        for k in range(1, n):
            copy = pltpu.make_async_remote_copy(
                src_ref=send.at[k - 1],
                dst_ref=recv.at[me],
                send_sem=wsend.at[w, k - 1],
                recv_sem=wrecv.at[w, k - 1],
                device_id=(targets[k], zz),
                device_id_type=MESH,
            )
            copy.start()
            copies.append(copy)
        sends.append(copies)

    def share(buffer, slot):
        copies = []
        for k in range(1, nb):
            copy = pltpu.make_async_remote_copy(
                src_ref=buffer.at[zz],
                dst_ref=buffer.at[zz],
                send_sem=zsend.at[slot, k - 1],
                recv_sem=zrecv.at[slot, k - 1],
                device_id=(me, lax.rem(zz + k, nb)),
                device_id_type=MESH,
            )
            copy.start()
            copies.append(copy)
        return copies

    label_all[zz] = labels_ref[...]
    label_copies = share(label_all, 5)

    for edge in (0, side + 1):
        wide[edge] = jnp.zeros(wide.shape[1:], BF16)
        wide[:, edge] = jnp.zeros((side + 2, images, mid), BF16)

    gain = blend([gain_ref[a : a + 1, :] for a in range(3)], own)
    bias = blend([bias_ref[a : a + 1, :] for a in range(3)], own)
    shift = blend([shift_ref[a : a + 1, :] for a in range(3)], own)

    def assemble(recv):
        value = recv[...]
        parts, depth, width = value.shape
        if depth % 16 == 0:
            return value.reshape(parts * depth, width)
        return value.astype(F32).reshape(parts * depth, width).astype(BF16)

    def finish(buffer):
        total = buffer[0]
        for z in range(1, nb):
            total = total + buffer[z]
        return total

    def scale_of(total, mean_out, var_out, low, high):
        mean = total[0:1] / count
        var = total[1:2] / count - mean * mean
        mean_out[...] = mean
        var_out[...] = var
        scale = lax.rsqrt(var + EPSILON) * gain[:, low:high]
        return scale, bias[:, low:high] - mean * scale

    for copy in sends[0]:
        copy.wait_recv()
    reduce_w = assemble(recv_r)
    for copy in act_copies:
        copy.wait()

    def reduce_step(b, carry):
        total, squares = carry
        x = act[pl.ds(b * step, step)].reshape(rows, cin)
        y = dot(x, reduce_w)
        rows_f32[b] = y
        return (
            total + jnp.sum(y, axis=0, keepdims=True),
            squares + jnp.sum(y * y, axis=0, keepdims=True),
        )

    zero = jnp.zeros((1, mid), F32)
    total, squares = lax.fori_loop(0, blocks, reduce_step, (zero, zero))
    stat1[zz, 0:1] = total
    stat1[zz, 1:2] = squares
    copies = share(stat1, 0)
    for copy in copies:
        copy.wait()
    scale1, offset1 = scale_of(finish(stat1), mean1_out, var1_out, 0, mid)

    def first_step(b, carry):
        y = jnp.maximum(rows_f32[b] * scale1 + offset1, 0.0)
        wide[pl.ds(b * step + 1, step), 1 : side + 1] = y.astype(BF16).reshape(
            step, side, images, mid
        )
        return carry

    lax.fori_loop(0, blocks, first_step, 0)

    for copy in sends[1]:
        copy.wait_recv()
    spatial_w = assemble(recv_s)

    def spatial_step(b, carry):
        total, squares = carry
        taps = [
            wide[pl.ds(b * step + dy, step), dx : dx + side].reshape(rows, mid)
            for dy in range(3)
            for dx in range(3)
        ]
        y = dot(jnp.concatenate(taps, axis=1), spatial_w)
        rows_f32[b] = y
        return (
            total + jnp.sum(y, axis=0, keepdims=True),
            squares + jnp.sum(y * y, axis=0, keepdims=True),
        )

    total, squares = lax.fori_loop(0, blocks, spatial_step, (zero, zero))
    stat2[zz, 0:1] = total
    stat2[zz, 1:2] = squares
    copies = share(stat2, 1)
    for copy in copies:
        copy.wait()
    scale2, offset2 = scale_of(finish(stat2), mean2_out, var2_out, mid, 2 * mid)

    def second_step(b, carry):
        gram, total = carry
        y = jnp.maximum(rows_f32[b] * scale2 + offset2, 0.0)
        y = y.astype(BF16)
        second[b] = y
        return (
            gram + dot(y, y, ((0,), (0,))),
            total + jnp.sum(y.astype(F32), axis=0, keepdims=True),
        )

    gram, total = lax.fori_loop(
        0, blocks, second_step, (jnp.zeros((mid, mid), F32), zero)
    )
    for copy in sends[2]:
        copy.wait_recv()
    expand_w = assemble(recv_e)

    def exact(a):
        high = a.astype(BF16)
        rest = a - high.astype(F32)
        middle = rest.astype(BF16)
        low = (rest - middle.astype(F32)).astype(BF16)
        return dot(high, expand_w) + (dot(middle, expand_w) + dot(low, expand_w))

    stat3[zz, 0:1] = exact(jnp.broadcast_to(total, (16, mid)))[0:1]
    stat3[zz, 1:2] = jnp.sum(exact(gram) * expand_w.astype(F32), axis=0, keepdims=True)
    copies = share(stat3, 2)
    for copy in copies:
        copy.wait()
    scale3, offset3 = scale_of(
        finish(stat3), mean3_out, var3_out, 2 * mid, 2 * mid + cin
    )

    area = side * images
    pooled_f32[...] = jnp.zeros_like(pooled_f32)

    def expand_step(i, carry):
        at = pl.ds(pl.multiple_of(lax.rem(i, step) * area, 16), area)
        x = second[i // step, at, :]
        wide_step = 256 if cin % 256 == 0 else cin
        for low in range(0, cin, wide_step):
            cut = slice(low, low + wide_step)
            e = dot(x, expand_w[:, cut]) * scale3[:, cut] + offset3[:, cut]
            e = e.reshape(side, images, wide_step) + act[i, :, :, cut].astype(F32)
            pooled_f32[:, cut] += jnp.sum(jnp.maximum(e, 0.0), axis=0)
        return carry

    lax.fori_loop(0, side, expand_step, 0)
    pooled_all[zz] = (pooled_f32[...] / float(side * side)).astype(BF16)
    copies = share(pooled_all, 3)
    for copy in sends[3]:
        copy.wait_recv()
    for copy in copies:
        copy.wait()
    for copy in label_copies:
        copy.wait()

    pooled = pooled_all[...].reshape(nb * images, cin)
    width = cin // n
    logits = None
    for q in range(n):
        term = dot(recv_c[q], pooled[:, q * width : (q + 1) * width], ((1,), (1,)))
        logits = term if logits is None else logits + term
    all_ids = lax.broadcasted_iota(jnp.int32, (chunk, classes), 1)
    own_ids = lax.broadcasted_iota(jnp.int32, (chunk, classes), 0) + start
    shift_column = jnp.sum(
        jnp.where(all_ids == own_ids, jnp.broadcast_to(shift, (chunk, classes)), 0.0),
        axis=1,
        keepdims=True,
    )
    logits = logits + shift_column
    class_ids = lax.broadcasted_iota(jnp.int32, (chunk, 1), 0) + start
    fresh = class_ids >= zz * chunk
    for z in range(nb):
        part = logits[:, z * images : (z + 1) * images]
        hit = class_ids == label_all[z]
        score[zz, z, 0:1] = jnp.sum(
            jnp.where(jnp.logical_and(hit, fresh), part, 0.0), axis=0, keepdims=True
        )
        score[zz, z, 1:2] = jnp.max(jnp.where(hit, -1e30, part), axis=0, keepdims=True)
    copies = share(score, 4)
    for copy in copies:
        copy.wait()
    correct = score[0, :, 0:1]
    rival = score[0, :, 1:2]
    for z in range(1, nb):
        correct = correct + score[z, :, 0:1]
        rival = jnp.maximum(rival, score[z, :, 1:2])
    margin = jnp.sum(jnp.sum(correct - rival, axis=2, keepdims=True), axis=0) / float(
        nb * images
    )
    margins[me] = jnp.broadcast_to(margin, margins.shape[1:])
    copies = []
    for k in range(1, n):
        copy = pltpu.make_async_remote_copy(
            src_ref=margins.at[me],
            dst_ref=margins.at[me],
            send_sem=msend.at[k - 1],
            recv_sem=mrecv.at[k - 1],
            device_id=(targets[k], zz),
            device_id_type=MESH,
        )
        copy.start()
        copies.append(copy)
    for group in sends:
        for copy in group:
            copy.wait_send()
    for copy in copies:
        copy.wait()
    lanes = lax.broadcasted_iota(jnp.int32, (1, 128), 1)
    result = jnp.zeros((1, 128), F32)
    for q in range(n):
        result = jnp.where(lanes == q, margins[q, 0:1, :], result)
    margin_out[...] = result


def shards(
    n,
    nb,
    activations,
    labels,
    t_values,
    point_index,
    w_reduce,
    w_spatial,
    w_expand,
    w_classes,
    norm_gain,
    norm_bias,
    class_bias,
):
    images, side, _, cin = activations.shape
    mid = w_reduce.shape[2]
    classes = w_classes.shape[1]
    chunk = round_up(-(-classes // nb), 16)
    step = block_of(side)
    blocks = side // step
    rows = step * side * images
    cfg = (n, nb, images, side, cin, mid, classes, chunk, step)
    smem = pl.BlockSpec(memory_space=pltpu.SMEM)
    vmem = pl.BlockSpec(memory_space=pltpu.VMEM)
    hbm = pl.BlockSpec(memory_space=pltpu.HBM)

    def slices(parts):
        return [
            pltpu.VMEM((parts,) + w_reduce.shape[1:], BF16),
            pltpu.VMEM((parts,) + w_spatial.shape[1:], BF16),
            pltpu.VMEM((parts,) + w_expand.shape[1:], BF16),
            pltpu.VMEM((parts, chunk, w_classes.shape[2]), BF16),
        ]

    dma = pltpu.SemaphoreType.DMA
    outs = pl.pallas_call(
        functools.partial(kernel, cfg),
        out_shape=[
            jax.ShapeDtypeStruct((1, mid), F32),
            jax.ShapeDtypeStruct((1, mid), F32),
            jax.ShapeDtypeStruct((1, mid), F32),
            jax.ShapeDtypeStruct((1, mid), F32),
            jax.ShapeDtypeStruct((1, cin), F32),
            jax.ShapeDtypeStruct((1, cin), F32),
            jax.ShapeDtypeStruct((1, 128), F32),
        ],
        in_specs=[smem, smem, vmem, vmem, vmem, vmem, hbm, hbm, hbm, hbm, hbm],
        out_specs=[vmem] * 7,
        scratch_shapes=[
            pltpu.VMEM((side, side, images, cin), BF16),
            *slices(3),
            *slices(n - 1),
            *slices(n),
            pltpu.VMEM((blocks, rows, mid), F32),
            pltpu.VMEM((side + 2, side + 2, images, mid), BF16),
            pltpu.VMEM((blocks, rows, mid), BF16),
            pltpu.VMEM((images, cin), F32),
            pltpu.VMEM((nb, images, cin), BF16),
            pltpu.VMEM((nb, 2, mid), F32),
            pltpu.VMEM((nb, 2, mid), F32),
            pltpu.VMEM((nb, 2, cin), F32),
            pltpu.VMEM((nb, 1, images), jnp.int32),
            pltpu.VMEM((nb, nb, 2, images), F32),
            pltpu.VMEM((n, 8, 128), F32),
            dma((4,)),
            dma((blocks,)),
            dma((4, n - 1)),
            dma((4, n - 1)),
            dma((6, nb - 1)),
            dma((6, nb - 1)),
            dma((n - 1,)),
            dma((n - 1,)),
        ],
        compiler_params=pltpu.CompilerParams(
            collective_id=0, has_side_effects=True, vmem_limit_bytes=62 * 1024 * 1024
        ),
    )(
        t_values,
        point_index,
        labels[None, :],
        norm_gain,
        norm_bias,
        class_bias,
        jnp.transpose(activations, (1, 2, 0, 3)),
        w_reduce,
        w_spatial,
        w_expand,
        w_classes,
    )
    return (*outs[:6], outs[6][0, : point_index.shape[0]])


def solution(mesh):
    n, nb = mesh.shape["point"], mesh.shape["batch"]
    placed = (
        P("batch", None, None, None),
        P("batch"),
        P(),
        P(),
        P(None, "point", None),
        P(None, "point", None),
        P(None, "point", None),
        P(None, None, "point"),
        P(),
        P(),
        P(),
    )
    return jax.shard_map(
        functools.partial(shards, n, nb),
        mesh=mesh,
        in_specs=placed,
        out_specs=(
            P("point", None),
            P("point", None),
            P("point", None),
            P("point", None),
            P("point", None),
            P("point", None),
            P(),
        ),
        check_vma=False,
    )
```

time: 209 us -> 77.5 us (0.37)
  blocking collectives: 71.7 us -> 0 us
  Pallas kernels: 0 us -> 68 us
  matrix products: 57.1 us -> 0 us
  other arithmetic: 32.2 us -> 0 us
  waiting for transfers between devices: 24.9 us -> 0 us
  between operations: 14.6 us -> 0.65 us
    psum x4 -> x0, blocking collectives: 71.7 us -> none  [the longest x1 39.6 us: shards(): margin_all = lax.psum(placed, ('point', 'batch'))]
    pallas_call x0 -> x1, Pallas kernels: none -> 68 us  [shards(): pl.pallas_call(functools.partial(kernel, cfg), out_shape=[jax.ShapeDtypeS...]
    dot_general x6 -> x0, matrix products: 57.1 us -> none  [the longest x5 51 us: map_product(): lax.dot_general(maps, kernel, (((3,), (0,)), ((), ())), preferred_element...]
    all_gather x4 -> x0, waiting for transfers between devices: 22.3 us -> none  [the longest x3 22.3 us: point_weight(): gathered = lax.all_gather(endpoints, 'point', axis=1, tiled=True)]
    reduce_sum x3 -> x0, other arithmetic: 16.3 us -> none  [the longest x1 14.9 us: shards(): pooled = jnp.mean(block_out, axis=(1, 2)).astype(jnp.bfloat16)]
    convert_element_type x2 -> x0, other arithmetic: 8.59 us -> none  [the longest x1 4.52 us: point_weight(): return blend_all(own_row, gathered)[0].astype(jnp.bfloat16)]
    add x2 -> x0, other arithmetic: 5.52 us -> none  [blend_all(): return start_part + bend_part + final_part]
    slice x6 -> x0, local copies, waits for them, and re-layouts: 5.5 us -> none  [the longest x1 4.94 us: spatial_conv(): padded[:, :, 0:side_len, :]]
  transfers between devices with their start and end apart: 4 -> 0, of which waited for: 2 -> 0; matrix products, arithmetic and copies ran while one was open for 42% -> 0% of each run, Pallas kernels for 0% -> 0%
where the time goes in v1:
time: 77.5 us; the launch traced here: 77.2 us
  Pallas kernels  68 us (88%)
  local copies, waits for them, and re-layouts  8.57 us (11%)
    pallas_call x1, Pallas kernels, shards(): pl.pallas_call(functools.partial(kernel, cfg), out_shape=[jax.ShapeDtypeS...  68 us
    unnamed x6, local copies, waits for them, and re-layouts  7.37 us

profile of v1, /device:TPU:0, one launch (start us, length us, event | category | flops | bytes accessed | tf_op | source)
XLA Modules:
  0.0 77.2 jit_solution(2687564741238930317)
XLA Ops:
  0.6 68.0 %shard_map.162 = (f32[1,256]{1,0:T(1,128)}, f32[1,256]{1,0:T(1,128)}, f32[1,256]{1,0:T(1,128)}, f32[1,256]{1,0:T(1,128)}, f32[1,1024]{1,0:T(1,128)}, /*index=5*/f32[1,1024]{1,0:T(1,128)}, f32[1,128]{1,0:T(1,128)}) custom-call(f32[64]{0:T(128)} %t_ref.1, s32[8]{0:T(128)} %index_ref.1, s32[1,32]{1,0:T(1,128)} %bitcast.5, f32[3,1536]{1,0:T(4,128)} %gain_ref.1, ...), custom_call_target="tpu_custom_call" | custom-call | tf_op jit(solution)/shard_map/pallas_call | solution.py:434
  68.6 1.2 %slice_bitcast_fusion = f32[8]{0:T(128)} fusion(f32[1,128]{1,0:T(1,128)} %get-tuple-element.20), kind=kLoop, calls=%fused_computation | loop fusion | bytes 64 | tf_op jit(solution)/shard_map/squeeze | solution.py:488
  69.8 1.2 %copy.24 = f32[1,256]{1,0:T(1,128)} copy(f32[1,256]{1,0:T(1,128)} %get-tuple-element.28) | data formatting | bytes 2048
  71.0 1.2 %copy.25 = f32[1,256]{1,0:T(1,128)} copy(f32[1,256]{1,0:T(1,128)} %get-tuple-element.29) | data formatting | bytes 2048
  72.2 1.2 %copy.26 = f32[1,256]{1,0:T(1,128)} copy(f32[1,256]{1,0:T(1,128)} %get-tuple-element.30) | data formatting | bytes 2048
  73.4 1.2 %copy.27 = f32[1,256]{1,0:T(1,128)} copy(f32[1,256]{1,0:T(1,128)} %get-tuple-element.31) | data formatting | bytes 2048
  74.7 1.3 %copy.28 = f32[1,1024]{1,0:T(1,128)} copy(f32[1,1024]{1,0:T(1,128)} %get-tuple-element.32) | data formatting | bytes 8192
  75.9 1.3 %copy.29 = f32[1,1024]{1,0:T(1,128)} copy(f32[1,1024]{1,0:T(1,128)} %get-tuple-element.33) | data formatting | bytes 8192

commit v2 on v1

--- a/solution.py
+++ b/solution.py
@@ -1,5 +1,4 @@
 import functools
-import math
 
 import jax
 import jax.numpy as jnp
@@ -12,10 +11,6 @@
 MESH = pl.DeviceIdType.MESH
 BF16 = jnp.bfloat16
 F32 = jnp.float32
-
-
-def round_up(value, step):
-    return (value + step - 1) // step * step
 
 
 def block_of(side):
@@ -63,12 +58,10 @@
     wide,
     second,
     pooled_f32,
-    pooled_all,
+    shift_col,
     stat1,
     stat2,
     stat3,
-    label_all,
-    score,
     margins,
     local_sem,
     act_sem,
@@ -79,24 +72,22 @@
     msend,
     mrecv,
 ):
-    n, nb, images, side, cin, mid, classes, chunk, step = cfg
+    n, nb, images, side, cin, mid, classes, step = cfg
     blocks = side // step
     rows = step * side * images
     me = lax.axis_index("point")
     zz = lax.axis_index("batch")
     count = float(images * side * side * nb)
-    start = jnp.minimum(zz * chunk, classes - chunk)
-    start = pl.multiple_of(start, 8)
+    others = [
+        (lax.rem(me + k, n), lax.rem(zz + j, nb))
+        for k in range(n)
+        for j in range(nb)
+        if k or j
+    ]
 
     barrier = pltpu.get_barrier_semaphore()
-    for k in range(1, n):
-        pl.semaphore_signal(
-            barrier, inc=1, device_id=(lax.rem(me + k, n), zz), device_id_type=MESH
-        )
-    for k in range(1, nb):
-        pl.semaphore_signal(
-            barrier, inc=1, device_id=(me, lax.rem(zz + k, nb)), device_id_type=MESH
-        )
+    for other in others:
+        pl.semaphore_signal(barrier, inc=1, device_id=other, device_id_type=MESH)
 
     anchor_copies = []
     for i, (src, dst) in enumerate(
@@ -104,7 +95,7 @@
             (wr_hbm, anchor_r),
             (ws_hbm, anchor_s),
             (we_hbm, anchor_e),
-            (wc_hbm.at[:, pl.ds(start, chunk), :], anchor_c),
+            (wc_hbm, anchor_c),
         )
     ):
         copy = pltpu.make_async_copy(src, dst, local_sem.at[i])
@@ -142,22 +133,28 @@
         (anchor_e, send_e, recv_e),
         (anchor_c, send_c, recv_c),
     )
-    for w, (anchor, send, recv) in enumerate(weights):
+
+    def blend_and_send(w):
+        anchor, send, recv = weights[w]
         anchor_copies[w].wait()
         total = anchor.shape[1]
-        piece = 32 if total % 32 == 0 else 8
-
-        def one(j, carry, anchor=anchor, send=send, recv=recv, piece=piece):
-            at = pl.ds(pl.multiple_of(j * piece, piece), piece)
+        piece = 64 if anchor.shape[2] <= 128 else 32
+
+        def part(at):
             ends = [anchor[a, at, :].astype(F32) for a in range(3)]
             for k in range(1, n):
                 send[k - 1, at, :] = blend(ends, coefs[k]).astype(BF16)
             recv[me, at, :] = blend(ends, own).astype(BF16)
+
+        def one(j, carry):
+            part(pl.ds(pl.multiple_of(j * piece, piece), piece))
             return carry
 
         lax.fori_loop(0, total // piece, one, 0)
+        if total % piece:
+            part(pl.ds(total - total % piece, total % piece))
         if w == 0:
-            pl.semaphore_wait(barrier, n - 1 + nb - 1)
+            pl.semaphore_wait(barrier, n * nb - 1)
         copies = []
         for k in range(1, n):
             copy = pltpu.make_async_remote_copy(
@@ -171,6 +168,9 @@
             copy.start()
             copies.append(copy)
         sends.append(copies)
+
+    for w in range(3):
+        blend_and_send(w)
 
     def share(buffer, slot):
         copies = []
@@ -187,9 +187,6 @@
             copies.append(copy)
         return copies
 
-    label_all[zz] = labels_ref[...]
-    label_copies = share(label_all, 5)
-
     for edge in (0, side + 1):
         wide[edge] = jnp.zeros(wide.shape[1:], BF16)
         wide[:, edge] = jnp.zeros((side + 2, images, mid), BF16)
@@ -218,6 +215,17 @@
         var_out[...] = var
         scale = lax.rsqrt(var + EPSILON) * gain[:, low:high]
         return scale, bias[:, low:high] - mean * scale
+
+    piece = 128
+    for low in range(0, classes, piece):
+        high = min(classes, low + piece)
+        size = high - low
+        square = lax.broadcasted_iota(jnp.int32, (size, size), 0) == (
+            lax.broadcasted_iota(jnp.int32, (size, size), 1)
+        )
+        shift_col[low:high, :] = jnp.sum(
+            jnp.where(square, shift[:, low:high], 0.0), axis=1, keepdims=True
+        )
 
     for copy in sends[0]:
         copy.wait_recv()
@@ -240,6 +248,7 @@
     stat1[zz, 0:1] = total
     stat1[zz, 1:2] = squares
     copies = share(stat1, 0)
+    blend_and_send(3)
     for copy in copies:
         copy.wait()
     scale1, offset1 = scale_of(finish(stat1), mean1_out, var1_out, 0, mid)
@@ -327,58 +336,35 @@
         return carry
 
     lax.fori_loop(0, side, expand_step, 0)
-    pooled_all[zz] = (pooled_f32[...] / float(side * side)).astype(BF16)
-    copies = share(pooled_all, 3)
+    pooled = (pooled_f32[...] / float(side * side)).astype(BF16)
     for copy in sends[3]:
         copy.wait_recv()
-    for copy in copies:
-        copy.wait()
-    for copy in label_copies:
-        copy.wait()
-
-    pooled = pooled_all[...].reshape(nb * images, cin)
+
     width = cin // n
-    logits = None
-    for q in range(n):
-        term = dot(recv_c[q], pooled[:, q * width : (q + 1) * width], ((1,), (1,)))
-        logits = term if logits is None else logits + term
-    all_ids = lax.broadcasted_iota(jnp.int32, (chunk, classes), 1)
-    own_ids = lax.broadcasted_iota(jnp.int32, (chunk, classes), 0) + start
-    shift_column = jnp.sum(
-        jnp.where(all_ids == own_ids, jnp.broadcast_to(shift, (chunk, classes)), 0.0),
-        axis=1,
-        keepdims=True,
-    )
-    logits = logits + shift_column
-    class_ids = lax.broadcasted_iota(jnp.int32, (chunk, 1), 0) + start
-    fresh = class_ids >= zz * chunk
-    for z in range(nb):
-        part = logits[:, z * images : (z + 1) * images]
-        hit = class_ids == label_all[z]
-        score[zz, z, 0:1] = jnp.sum(
-            jnp.where(jnp.logical_and(hit, fresh), part, 0.0), axis=0, keepdims=True
-        )
-        score[zz, z, 1:2] = jnp.max(jnp.where(hit, -1e30, part), axis=0, keepdims=True)
-    copies = share(score, 4)
-    for copy in copies:
-        copy.wait()
-    correct = score[0, :, 0:1]
-    rival = score[0, :, 1:2]
-    for z in range(1, nb):
-        correct = correct + score[z, :, 0:1]
-        rival = jnp.maximum(rival, score[z, :, 1:2])
-    margin = jnp.sum(jnp.sum(correct - rival, axis=2, keepdims=True), axis=0) / float(
-        nb * images
-    )
-    margins[me] = jnp.broadcast_to(margin, margins.shape[1:])
+    if width % 128 == 0:
+        class_w = jnp.concatenate([recv_c[q] for q in range(n)], axis=1)
+        logits = dot(class_w, pooled, ((1,), (1,)))
+    else:
+        logits = jnp.zeros((classes, images), F32)
+        for q in range(n):
+            part = pooled[:, q * width : (q + 1) * width]
+            logits = logits + dot(recv_c[q], part, ((1,), (1,)))
+    logits = logits + shift_col[...]
+    class_ids = lax.broadcasted_iota(jnp.int32, (classes, images), 0)
+    hit = class_ids == labels_ref[...]
+    correct = jnp.sum(jnp.where(hit, logits, 0.0), axis=0, keepdims=True)
+    rival = jnp.max(jnp.where(hit, -1e30, logits), axis=0, keepdims=True)
+    margin = jnp.sum(correct - rival, axis=1, keepdims=True) / float(nb * images)
+    mine = me * nb + zz
+    margins[mine] = jnp.broadcast_to(margin, margins.shape[1:])
     copies = []
-    for k in range(1, n):
+    for i, other in enumerate(others):
         copy = pltpu.make_async_remote_copy(
-            src_ref=margins.at[me],
-            dst_ref=margins.at[me],
-            send_sem=msend.at[k - 1],
-            recv_sem=mrecv.at[k - 1],
-            device_id=(targets[k], zz),
+            src_ref=margins.at[mine],
+            dst_ref=margins.at[mine],
+            send_sem=msend.at[i],
+            recv_sem=mrecv.at[i],
+            device_id=other,
             device_id_type=MESH,
         )
         copy.start()
@@ -391,8 +377,18 @@
     lanes = lax.broadcasted_iota(jnp.int32, (1, 128), 1)
     result = jnp.zeros((1, 128), F32)
     for q in range(n):
-        result = jnp.where(lanes == q, margins[q, 0:1, :], result)
+        part = margins[q * nb]
+        for z in range(1, nb):
+            part = part + margins[q * nb + z]
+        result = jnp.where(lanes == q, part, result)
     margin_out[...] = result
+
+
+def hand_over(*refs):
+    for source, target in zip(refs[:6], refs[7:13]):
+        target[...] = source[...]
+    points = refs[13].shape[0]
+    refs[13][...] = refs[6][0, 0:points]
 
 
 def shards(
@@ -413,11 +409,10 @@
     images, side, _, cin = activations.shape
     mid = w_reduce.shape[2]
     classes = w_classes.shape[1]
-    chunk = round_up(-(-classes // nb), 16)
     step = block_of(side)
     blocks = side // step
     rows = step * side * images
-    cfg = (n, nb, images, side, cin, mid, classes, chunk, step)
+    cfg = (n, nb, images, side, cin, mid, classes, step)
     smem = pl.BlockSpec(memory_space=pltpu.SMEM)
     vmem = pl.BlockSpec(memory_space=pltpu.VMEM)
     hbm = pl.BlockSpec(memory_space=pltpu.HBM)
@@ -427,7 +422,7 @@
             pltpu.VMEM((parts,) + w_reduce.shape[1:], BF16),
             pltpu.VMEM((parts,) + w_spatial.shape[1:], BF16),
             pltpu.VMEM((parts,) + w_expand.shape[1:], BF16),
-            pltpu.VMEM((parts, chunk, w_classes.shape[2]), BF16),
+            pltpu.VMEM((parts,) + w_classes.shape[1:], BF16),
         ]
 
     dma = pltpu.SemaphoreType.DMA
@@ -453,21 +448,19 @@
             pltpu.VMEM((side + 2, side + 2, images, mid), BF16),
             pltpu.VMEM((blocks, rows, mid), BF16),
             pltpu.VMEM((images, cin), F32),
-            pltpu.VMEM((nb, images, cin), BF16),
+            pltpu.VMEM((classes, 1), F32),
             pltpu.VMEM((nb, 2, mid), F32),
             pltpu.VMEM((nb, 2, mid), F32),
             pltpu.VMEM((nb, 2, cin), F32),
-            pltpu.VMEM((nb, 1, images), jnp.int32),
-            pltpu.VMEM((nb, nb, 2, images), F32),
-            pltpu.VMEM((n, 8, 128), F32),
+            pltpu.VMEM((n * nb, 1, 128), F32),
             dma((4,)),
             dma((blocks,)),
             dma((4, n - 1)),
             dma((4, n - 1)),
-            dma((6, nb - 1)),
-            dma((6, nb - 1)),
-            dma((n - 1,)),
-            dma((n - 1,)),
+            dma((3, nb - 1)),
+            dma((3, nb - 1)),
+            dma((n * nb - 1,)),
+            dma((n * nb - 1,)),
         ],
         compiler_params=pltpu.CompilerParams(
             collective_id=0, has_side_effects=True, vmem_limit_bytes=62 * 1024 * 1024
@@ -485,7 +478,14 @@
         w_expand,
         w_classes,
     )
-    return (*outs[:6], outs[6][0, : point_index.shape[0]])
+    points = point_index.shape[0]
+    return pl.pallas_call(
+        hand_over,
+        out_shape=[jax.ShapeDtypeStruct(o.shape, F32) for o in outs[:6]]
+        + [jax.ShapeDtypeStruct((points,), F32)],
+        in_specs=[vmem] * 7,
+        out_specs=[vmem] * 7,
+    )(*outs)
 
 
 def solution(mesh):

time: 77.5 us -> 64.1 us (0.83)
  local copies, waits for them, and re-layouts: 8.57 us -> 0 us
  Pallas kernels: 68 us -> 63.2 us
    unnamed x6 -> x0, local copies, waits for them, and re-layouts: 7.37 us -> none
    pallas_call x1, Pallas kernels: 68 us -> 61.9 us  [shards(): pl.pallas_call(functools.partial(kernel, cfg), out_shape=[jax.ShapeDtypeS...]
    pallas_call x0 -> x1, Pallas kernels: none -> 1.33 us  [shards(): pl.pallas_call(hand_over, out_shape=[jax.ShapeDtypeStruct(o.shape, F32) f...]
    squeeze x1 -> x0, local copies, waits for them, and re-layouts: 1.19 us -> none  [shards(): return (*outs[:6], outs[6][0, :point_index.shape[0]])]
where the time goes in v2:
time: 64.1 us; the launch traced here: 63.9 us
  Pallas kernels  63.2 us (99%)
    pallas_call x1, Pallas kernels, shards(): pl.pallas_call(functools.partial(kernel, cfg), out_shape=[jax.ShapeDtypeS...  61.9 us
    pallas_call x1, Pallas kernels, shards(): pl.pallas_call(hand_over, out_shape=[jax.ShapeDtypeStruct(o.shape, F32) f...  1.33 us

profile of v2, /device:TPU:0, one launch (start us, length us, event | category | flops | bytes accessed | tf_op | source)
XLA Modules:
  0.0 63.9 jit_solution(11838080295245514737)
XLA Ops:
  0.6 61.9 %shard_map.162 = (f32[1,256]{1,0:T(1,128)}, f32[1,256]{1,0:T(1,128)}, f32[1,256]{1,0:T(1,128)}, f32[1,256]{1,0:T(1,128)}, f32[1,1024]{1,0:T(1,128)}, /*index=5*/f32[1,1024]{1,0:T(1,128)}, f32[1,128]{1,0:T(1,128)}) custom-call(f32[64]{0:T(128)} %t_ref.1, s32[8]{0:T(128)} %index_ref.1, s32[1,32]{1,0:T(1,128)} %bitcast.3, f32[3,1536]{1,0:T(4,128)} %gain_ref.1, ...), custom_call_target="tpu_custom_call" | custom-call | tf_op jit(solution)/shard_map/pallas_call | solution.py:429
  62.5 1.3 %shard_map.163 = (f32[1,256]{1,0:T(1,128)}, f32[1,256]{1,0:T(1,128)}, f32[1,256]{1,0:T(1,128)}, f32[1,256]{1,0:T(1,128)}, f32[1,1024]{1,0:T(1,128)}, /*index=5*/f32[1,1024]{1,0:T(1,128)}, f32[8]{0:T(128)}) custom-call(f32[1,256]{1,0:T(1,128)} %get-tuple-element.14.refs_0_, f32[1,256]{1,0:T(1,128)} %get-tuple-element.15.refs_1_, ...), custom_call_target="tpu_custom_call" | custom-call | tf_op jit(solution)/shard_map/pallas_call | solution.py:482

commit v3 on v2

--- a/solution.py
+++ b/solution.py
@@ -67,6 +67,7 @@
     act_sem,
     wsend,
     wrecv,
+    pair,
     zsend,
     zrecv,
     msend,
@@ -134,6 +135,14 @@
         (anchor_c, send_c, recv_c),
     )
 
+    half = classes // 4 // 64 * 64 + 64 if nb % 2 == 0 else 0
+    low_bit = lax.rem(zz, 2)
+    mine_low = pl.multiple_of(low_bit * half, 8)
+    rest_rows = pl.ds(2 * half, classes - 2 * half)
+
+    def whole(w):
+        return pl.ds(0, weights[w][0].shape[1])
+
     def blend_and_send(w):
         anchor, send, recv = weights[w]
         anchor_copies[w].wait()
@@ -146,28 +155,55 @@
                 send[k - 1, at, :] = blend(ends, coefs[k]).astype(BF16)
             recv[me, at, :] = blend(ends, own).astype(BF16)
 
-        def one(j, carry):
-            part(pl.ds(pl.multiple_of(j * piece, piece), piece))
-            return carry
-
-        lax.fori_loop(0, total // piece, one, 0)
-        if total % piece:
-            part(pl.ds(total - total % piece, total % piece))
+        pieces = []
+        if w < 3:
+            spans = ((0, total),)
+            pieces.append((w, whole(w)))
+        else:
+            spans = ((mine_low, half), (2 * half, total - 2 * half))
+            if half:
+                pieces.append((3, pl.ds(mine_low, half)))
+            pieces.append((4, rest_rows))
+        for low, size in spans:
+
+            def one(j, carry):
+                part(pl.ds(pl.multiple_of(low + j * piece, 8), piece))
+                return carry
+
+            lax.fori_loop(0, size // piece, one, 0)
+            if size % piece:
+                part(pl.ds(low + size - size % piece, size % piece))
         if w == 0:
             pl.semaphore_wait(barrier, n * nb - 1)
-        copies = []
+        for slot, at in pieces:
+            copies = []
+            for k in range(n - 1, 0, -1):
+                copy = pltpu.make_async_remote_copy(
+                    src_ref=send.at[k - 1, at],
+                    dst_ref=recv.at[me, at],
+                    send_sem=wsend.at[slot, k],
+                    recv_sem=wrecv.at[slot, me],
+                    device_id=(targets[k], zz),
+                    device_id_type=MESH,
+                )
+                copy.start()
+                copies.append(copy)
+            sends.append(copies)
+
+    def arrived(slot, sender, at):
+        recv = weights[min(slot, 3)][2]
+        pltpu.make_async_remote_copy(
+            src_ref=recv.at[sender, at],
+            dst_ref=recv.at[sender, at],
+            send_sem=wsend.at[slot, 0],
+            recv_sem=wrecv.at[slot, sender],
+            device_id=(targets[1], zz),
+            device_id_type=MESH,
+        ).wait_recv()
+
+    def all_arrived(slot, at):
         for k in range(1, n):
-            copy = pltpu.make_async_remote_copy(
-                src_ref=send.at[k - 1],
-                dst_ref=recv.at[me],
-                send_sem=wsend.at[w, k - 1],
-                recv_sem=wrecv.at[w, k - 1],
-                device_id=(targets[k], zz),
-                device_id_type=MESH,
-            )
-            copy.start()
-            copies.append(copy)
-        sends.append(copies)
+            arrived(slot, targets[k], at)
 
     for w in range(3):
         blend_and_send(w)
@@ -227,24 +263,38 @@
             jnp.where(square, shift[:, low:high], 0.0), axis=1, keepdims=True
         )
 
-    for copy in sends[0]:
-        copy.wait_recv()
-    reduce_w = assemble(recv_r)
     for copy in act_copies:
         copy.wait()
-
-    def reduce_step(b, carry):
-        total, squares = carry
-        x = act[pl.ds(b * step, step)].reshape(rows, cin)
-        y = dot(x, reduce_w)
-        rows_f32[b] = y
-        return (
-            total + jnp.sum(y, axis=0, keepdims=True),
-            squares + jnp.sum(y * y, axis=0, keepdims=True),
-        )
-
+    per = max(1, min(n, 256 * n // cin))
+    groups = n // per
+    deep = cin // groups
     zero = jnp.zeros((1, mid), F32)
-    total, squares = lax.fori_loop(0, blocks, reduce_step, (zero, zero))
+    total, squares = zero, zero
+    for j in range(groups):
+        group = lax.rem(lax.div(me, per) + j, groups)
+        for i in range(per):
+            if j == 0 and i == 0:
+                continue
+            member = lax.rem(lax.rem(me, per) + i, per)
+            arrived(0, group * per + member, whole(0))
+        reduce_w = assemble(recv_r.at[pl.ds(group * per, per)])
+        columns = pl.ds(pl.multiple_of(group * deep, 128), deep)
+
+        def reduce_step(b, carry):
+            total, squares = carry
+            x = act[pl.ds(b * step, step), :, :, columns].reshape(rows, deep)
+            y = dot(x, reduce_w)
+            if j > 0:
+                y = y + rows_f32[b]
+            rows_f32[b] = y
+            if j < groups - 1:
+                return carry
+            return (
+                total + jnp.sum(y, axis=0, keepdims=True),
+                squares + jnp.sum(y * y, axis=0, keepdims=True),
+            )
+
+        total, squares = lax.fori_loop(0, blocks, reduce_step, (total, squares))
     stat1[zz, 0:1] = total
     stat1[zz, 1:2] = squares
     copies = share(stat1, 0)
@@ -262,8 +312,7 @@
 
     lax.fori_loop(0, blocks, first_step, 0)
 
-    for copy in sends[1]:
-        copy.wait_recv()
+    all_arrived(1, whole(1))
     spatial_w = assemble(recv_s)
 
     def spatial_step(b, carry):
@@ -288,6 +337,21 @@
         copy.wait()
     scale2, offset2 = scale_of(finish(stat2), mean2_out, var2_out, mid, 2 * mid)
 
+    passed = []
+    if half:
+        all_arrived(3, pl.ds(mine_low, half))
+        block = recv_c.at[:, pl.ds(mine_low, half), :]
+        copy = pltpu.make_async_remote_copy(
+            src_ref=block,
+            dst_ref=block,
+            send_sem=pair.at[0],
+            recv_sem=pair.at[1],
+            device_id=(me, zz + 1 - 2 * low_bit),
+            device_id_type=MESH,
+        )
+        copy.start()
+        passed.append(copy)
+
     def second_step(b, carry):
         gram, total = carry
         y = jnp.maximum(rows_f32[b] * scale2 + offset2, 0.0)
@@ -301,8 +365,7 @@
     gram, total = lax.fori_loop(
         0, blocks, second_step, (jnp.zeros((mid, mid), F32), zero)
     )
-    for copy in sends[2]:
-        copy.wait_recv()
+    all_arrived(2, whole(2))
     expand_w = assemble(recv_e)
 
     def exact(a):
@@ -337,8 +400,9 @@
 
     lax.fori_loop(0, side, expand_step, 0)
     pooled = (pooled_f32[...] / float(side * side)).astype(BF16)
-    for copy in sends[3]:
-        copy.wait_recv()
+    all_arrived(4, rest_rows)
+    for copy in passed:
+        copy.wait()
 
     width = cin // n
     if width % 128 == 0:
@@ -455,8 +519,9 @@
             pltpu.VMEM((n * nb, 1, 128), F32),
             dma((4,)),
             dma((blocks,)),
-            dma((4, n - 1)),
-            dma((4, n - 1)),
+            dma((5, n)),
+            dma((5, n)),
+            dma((2,)),
             dma((3, nb - 1)),
             dma((3, nb - 1)),
             dma((n * nb - 1,)),

time: 64.1 us -> 70 us (1.092)
  Pallas kernels: 63.2 us -> 69.2 us
    pallas_call x1, Pallas kernels: 61.9 us -> 67.8 us  [shards(): pl.pallas_call(functools.partial(kernel, cfg), out_shape=[jax.ShapeDtypeS...]
where the time goes in v3:
time: 70 us; the launch traced here: 69.8 us
  Pallas kernels  69.2 us (99%)
    pallas_call x1, Pallas kernels, shards(): pl.pallas_call(functools.partial(kernel, cfg), out_shape=[jax.ShapeDtypeS...  67.8 us

profile of v3, /device:TPU:0, one launch (start us, length us, event | category | flops | bytes accessed | tf_op | source)
XLA Modules:
  0.0 69.8 jit_solution(9696945006502243861)
XLA Ops:
  0.6 67.8 %shard_map.162 = (f32[1,256]{1,0:T(1,128)}, f32[1,256]{1,0:T(1,128)}, f32[1,256]{1,0:T(1,128)}, f32[1,256]{1,0:T(1,128)}, f32[1,1024]{1,0:T(1,128)}, /*index=5*/f32[1,1024]{1,0:T(1,128)}, f32[1,128]{1,0:T(1,128)}) custom-call(f32[64]{0:T(128)} %t_ref.1, s32[8]{0:T(128)} %index_ref.1, s32[1,32]{1,0:T(1,128)} %bitcast.3, f32[3,1536]{1,0:T(4,128)} %gain_ref.1, ...), custom_call_target="tpu_custom_call" | custom-call | tf_op jit(solution)/shard_map/pallas_call | solution.py:493
  68.5 1.3 %shard_map.163 = (f32[1,256]{1,0:T(1,128)}, f32[1,256]{1,0:T(1,128)}, f32[1,256]{1,0:T(1,128)}, f32[1,256]{1,0:T(1,128)}, f32[1,1024]{1,0:T(1,128)}, /*index=5*/f32[1,1024]{1,0:T(1,128)}, f32[8]{0:T(128)}) custom-call(f32[1,256]{1,0:T(1,128)} %get-tuple-element.14.refs_0_, f32[1,256]{1,0:T(1,128)} %get-tuple-element.15.refs_1_, ...), custom_call_target="tpu_custom_call" | custom-call | tf_op jit(solution)/shard_map/pallas_call | solution.py:547
